TPU v7x, 32 devices: a whole 2x2x4 slice. The times are simulated.
32 devices in a mesh: band: 16 (over z, y, x), dp: 2 (over core).
Axes of the slice: x: 2, y: 2, z: 4, core: 2. Of those that a mesh axis runs over, the one named last changes fastest.
Arguments:
- pages: bfloat16 [32768, 256], P('band', 'dp'), may hold values from -6 to 6
- band_tiles: bfloat16 [256, 3, 128, 128], P('band'), may hold values from 0 to 1, as said below
- off_tiles: bfloat16 [256, 128, 128], P('band'), may hold values from 0 to 1, as said below
- off_row: int32 [256], P('band'), may hold values from 0 to 15
- requests: int32 [256], P('band'), may hold values from 0 to 15
- label_page: int32 [16384], P('band'), may hold values from 0 to 2047
- labels: int32 [16384], P(('band', 'dp')), may hold values from 0 to 255
- w_first: bfloat16 [768, 1024], replicated, may hold values from -0.21875 to 0.21875
- w_second: bfloat16 [1024, 256], replicated
Outputs:
- prop_a: bfloat16 [32768, 256], P('band', 'dp')
- prop_t: bfloat16 [32768, 256], P('band', 'dp')
- prop_aat: bfloat16 [32768, 256], P('band', 'dp')
- grad_w1: bfloat16 [768, 1024], replicated
- grad_w2: bfloat16 [1024, 256], replicated
Inputs may be any that keep to these rules, and one draw needn't show every extreme that they name: `off_row`: row block within a band. `requests`: row block within a band. `band_tiles`: links weighted between 0 and 1, about half of the entries zero. `off_tiles`: links weighted between 0 and 1, about half of the entries zero.
All inputs are finite; a program needn't handle non-finite values.
Results may differ from a plain program's by a relative error of at most 0.011.
Values may be sent and summed in bfloat16 or wider, within the bound.
A program may use at most 128 MiB of HBM per device.

v0:
```python
import jax
import jax.numpy as jnp
from jax import lax
from jax.sharding import PartitionSpec as P


def padded_2(cells, sides, width):
    for axis, dim in sides:
        count = lax.axis_size(axis)
        ends = count - 1
        head = lax.slice_in_dim(cells, 0, width, axis=dim)
        tail = lax.slice_in_dim(cells, cells.shape[dim] - width, cells.shape[dim], axis=dim)
        cells = jnp.concatenate(
            [
                lax.ppermute(tail, axis, [(i, (i + 1) % count) for i in range(ends)]),
                cells,
                lax.ppermute(head, axis, [((i + 1) % count, i) for i in range(ends)]),
            ],
            axis=dim,
        )
    return cells


def per_device(
    pages, band_tiles, off_tiles, off_row, requests, label_page, labels, w_first, w_second
):
    tile_size = band_tiles.shape[-1]
    rows_dev, feat_half = pages.shape
    block_count = rows_dev // tile_size
    block_iota = jnp.arange(block_count, dtype=jnp.int32)
    served = lax.all_to_all(requests, "band", split_axis=0, concat_axis=0, tiled=True)
    row_hot = (off_row[None, :] == block_iota[:, None]).astype(jnp.float32)
    served_hot = (served[None, :] == block_iota[:, None]).astype(jnp.float32)

    def band_forward(field):
        padded = padded_2(field, (("band", 0),), tile_size)
        blocks = padded.reshape(block_count + 2, tile_size, feat_half)
        windows = jnp.stack(
            [blocks[0:block_count], blocks[1 : block_count + 1], blocks[2 : block_count + 2]], 1
        )
        return jnp.einsum("rjab,rjbf->raf", band_tiles, windows, preferred_element_type=jnp.float32)

    def off_apply(fetched):
        products = jnp.einsum(
            "kab,kbf->kaf", off_tiles, fetched, preferred_element_type=jnp.float32
        )
        return jnp.einsum("rk,kaf->raf", row_hot, products, precision=lax.Precision.HIGHEST)

    def serve_blocks(field):
        return jnp.take(field.reshape(block_count, tile_size, feat_half), served, axis=0)

    own_blocks = pages.reshape(block_count, tile_size, feat_half)
    near_part = band_forward(pages)
    adjoint_terms = jnp.einsum(
        "rjab,raf->rjbf", band_tiles, own_blocks, preferred_element_type=jnp.float32
    )
    accumulated = jnp.zeros((block_count + 2, tile_size, feat_half), jnp.float32)
    accumulated = accumulated.at[0:block_count].add(adjoint_terms[:, 0])
    accumulated = accumulated.at[1 : block_count + 1].add(adjoint_terms[:, 1])
    accumulated = accumulated.at[2 : block_count + 2].add(adjoint_terms[:, 2])
    rim_rows = jnp.concatenate([accumulated[0], accumulated[block_count + 1]], 0)
    received = padded_2(rim_rows, (("band", 0),), tile_size)
    inner_part = accumulated[1 : block_count + 1]
    inner_part = inner_part.at[0].add(received[0:tile_size])
    inner_part = inner_part.at[block_count - 1].add(received[3 * tile_size : 4 * tile_size])
    back_terms = jnp.einsum(
        "kab,kaf->kbf",
        off_tiles,
        jnp.take(own_blocks, off_row, axis=0),
        preferred_element_type=jnp.float32,
    ).astype(jnp.bfloat16)
    outgoing = serve_blocks(pages)
    fetched = lax.all_to_all(outgoing, "band", split_axis=0, concat_axis=0, tiled=True)
    returned = lax.all_to_all(back_terms, "band", split_axis=0, concat_axis=0, tiled=True)
    prop_a = (near_part + off_apply(fetched)).reshape(rows_dev, feat_half).astype(jnp.bfloat16)
    back_sum = jnp.einsum(
        "rk,kbf->rbf", served_hot, returned.astype(jnp.float32), precision=lax.Precision.HIGHEST
    )
    prop_t = (inner_part + back_sum).reshape(rows_dev, feat_half).astype(jnp.bfloat16)
    fetched_again = lax.all_to_all(
        serve_blocks(prop_t), "band", split_axis=0, concat_axis=0, tiled=True
    )
    prop_aat = (
        (band_forward(prop_t) + off_apply(fetched_again))
        .reshape(rows_dev, feat_half)
        .astype(jnp.bfloat16)
    )
    picked = jnp.stack(
        [
            jnp.take(prop_a, label_page, axis=0),
            jnp.take(prop_t, label_page, axis=0),
            jnp.take(prop_aat, label_page, axis=0),
        ],
        0,
    )
    regrouped = lax.all_to_all(picked, "dp", split_axis=1, concat_axis=2, tiled=True)
    hidden_units = w_first.shape[1]
    w_first_split = w_first.reshape(3, regrouped.shape[2], hidden_units)
    pre_act = jnp.einsum(
        "krf,kfh->rh", regrouped, w_first_split, preferred_element_type=jnp.float32
    )
    sigma = jax.nn.sigmoid(pre_act)
    hidden = (pre_act * sigma).astype(jnp.bfloat16)
    logits = jnp.dot(hidden, w_second, preferred_element_type=jnp.float32)
    probabilities = jax.nn.softmax(logits, axis=-1)
    label_hot = (labels[:, None] == jnp.arange(w_second.shape[1], dtype=jnp.int32)[None, :]).astype(
        jnp.float32
    )
    errors = ((probabilities - label_hot) / label_page.shape[0]).astype(jnp.bfloat16)
    grad_second = jnp.dot(hidden.T, errors, preferred_element_type=jnp.float32)
    slope = sigma * (1.0 + pre_act * (1.0 - sigma))
    back_signal = (jnp.dot(errors, w_second.T, preferred_element_type=jnp.float32) * slope).astype(
        jnp.bfloat16
    )
    grad_first = jnp.einsum(
        "krf,rh->kfh", regrouped, back_signal, preferred_element_type=jnp.float32
    ).reshape(w_first.shape[0], hidden_units)
    summed_first, summed_second = lax.psum((grad_first, grad_second), ("band", "dp"))
    return (
        prop_a,
        prop_t,
        prop_aat,
        summed_first.astype(jnp.bfloat16),
        summed_second.astype(jnp.bfloat16),
    )


def solution(mesh):
    placed = (
        P("band", "dp"),
        P("band", None, None, None),
        P("band", None, None),
        P("band"),
        P("band"),
        P("band"),
        P(("band", "dp")),
        P(),
        P(),
    )
    return jax.shard_map(
        per_device,
        mesh=mesh,
        in_specs=placed,
        out_specs=(P("band", "dp"), P("band", "dp"), P("band", "dp"), P(), P()),
        check_vma=False,
    )
```

profile of v0, /device:TPU:0, one launch (start us, length us, event | category | flops | bytes accessed | tf_op | source)
XLA Modules:
  0.0 221.8 jit_solution(7156766890405385631)
XLA Ops:
  0.6 1.4 copy.47
  2.1 8.3 %all-to-all-start = ((s32[16,1,1]{2,1,0:T(1,128)}), s32[16,1,1]{2,1,0:T(1,128)S(1)}, u32[]{:S(2)}, u32[]{:S(2)}) async-start(s32[16,1,1]{2,1,0:T(1,128)} %copy.47), calls=%async_computation | async-start | bytes 16384 | tf_op jit(solution)/shard_map/all_to_all | solution.py:31
  11.2 3.8 %collective-permute-start = (bf16[128,128]{1,0:T(8,128)(2,1)S(1)}, bf16[128,128]{1,0:T(8,128)(2,1)S(1)}, u32[]{:S(2)}, u32[]{:S(2)}) collective-permute-start(bf16[128,128]{1,0:T(8,128)(2,1)S(1)} %get-tuple-element.77), channel_id=1, source_target_pairs={{0,2},{2,4},{4,6},{6,8},{8,10},{10,12},{12,14},{14,16},{16,18},{18... | collective-permute-start | bytes 98312 | tf_op jit(solution)/shard_map/ppermute | solution.py:15
  16.3 2.1 fusion.78
  19.1 4.5 %collective-permute-start.2 = (f32[128,128]{1,0:T(8,128)S(1)}, f32[128,128]{1,0:T(8,128)S(1)}, u32[]{:S(2)}, u32[]{:S(2)}) collective-permute-start(f32[128,128]{1,0:T(8,128)S(1)} %slice_bitcast_fusion.4), channel_id=1, source_target_pairs={{0,2},{2,4},{4,6},{6,8},{8,10},{10,12},{12,14},{14,16},{16,18},{18... | collective-permute-start | bytes 196616 | tf_op jit(solution)/shard_map/ppermute | solution.py:15
  26.3 2.4 %fusion.46 = bf16[16,128,128]{1,2,0:T(8,128)(2,1)} fusion(bf16[16,128,128]{2,1,0:T(8,128)(2,1)} %param.25, bf16[16,128,128]{2,1,0:T(8,128)(2,1)} %gather_fusion.1, pred[16]{0:T(512)(128)(4,1)} %compare_and_fusion.1), kind=kOutput, calls=%fused_computation.40 | convolution fusion | flops 67633152 | bytes 1572880 | tf_op jit(solution)/shard_map/kab,kaf->kbf/dot_general | solution.py:66
  28.8 2.0 copy.55
  31.9 7.4 %all-to-all-start.2 = ((bf16[16,128,128]{2,1,0:T(8,128)(2,1)}), bf16[16,128,128]{2,1,0:T(8,128)(2,1)}, u32[]{:S(2)}, u32[]{:S(2)}) async-start(bf16[16,128,128]{2,1,0:T(8,128)(2,1)} %copy.55), calls=%async_computation.2 | async-start | bytes 1048576 | tf_op jit(solution)/shard_map/all_to_all | solution.py:74
  42.9 2.0 copy.48
  44.9 1.9 broadcast_select_fusion.1
  49.9 3.8 %collective-permute-done.3 = f32[128,128]{1,0:T(8,128)S(1)} collective-permute-done((f32[128,128]{1,0:T(8,128)S(1)}, f32[128,128]{1,0:T(8,128)S(1)}, u32[]{:S(2)}, u32[]{:S(2)}) %collective-permute-start.3) | collective-permute-done | bytes 65568 | tf_op jit(solution)/shard_map/ppermute | solution.py:17
  53.7 1.5 fusion.58
  55.1 7.8 %all-to-all-start.1 = ((bf16[16,128,128]{1,2,0:T(8,128)(2,1)}), bf16[16,128,128]{1,2,0:T(8,128)(2,1)}, u32[]{:S(2)}, u32[]{:S(2)}) async-start(bf16[16,128,128]{1,2,0:T(8,128)(2,1)} %broadcast_select_fusion.1), calls=%async_computation.1 | async-start | bytes 1048576 | tf_op jit(solution)/shard_map/all_to_all | solution.py:73
  63.0 1.5 fusion.52
  66.3 3.8 %collective-permute-start.4 = (bf16[128,128]{1,0:T(8,128)(2,1)S(1)}, bf16[128,128]{1,0:T(8,128)(2,1)S(1)}, u32[]{:S(2)}, u32[]{:S(2)}) collective-permute-start(bf16[128,128]{1,0:T(8,128)(2,1)S(1)} %get-tuple-element.73), channel_id=1, source_target_pairs={{0,2},{2,4},{4,6},{6,8},{8,10},{10,12},{12,14},{14,16},{16,18},{18... | collective-permute-start | bytes 98312 | tf_op jit(solution)/shard_map/ppermute | solution.py:15
  71.4 3.2 %gather_fusion.4 = bf16[1024,128]{1,0:T(8,128)(2,1)S(1)} fusion(bf16[2048,128]{1,0:T(8,128)(2,1)S(1)} %bitcast.130, s32[1024]{0:T(1024)S(1)} %fusion.70), kind=kCustom, calls=%fused_computation.4.clone | custom fusion | bytes 528384 | tf_op jit(solution)/shard_map/jit(_take)/gather | solution.py:91
  74.6 2.0 broadcast_select_fusion
  76.6 7.7 %all-to-all-start.3 = ((bf16[16,128,128]{2,1,0:T(8,128)(2,1)}), bf16[16,128,128]{2,1,0:T(8,128)(2,1)}, u32[]{:S(2)}, u32[]{:S(2)}) async-start(bf16[16,128,128]{2,1,0:T(8,128)(2,1)} %broadcast_select_fusion), calls=%async_computation.3 | async-start | bytes 1048576 | tf_op jit(solution)/shard_map/all_to_all | solution.py:80
  84.3 2.5 %convolution_bitcast_fusion.1 = f32[16,128,128]{1,2,0:T(8,128)} fusion(bf16[16,128,128]{1,2,0:T(8,128)(2,1)} %all-to-all-done.1, bf16[16,128,128]{2,1,0:T(8,128)(2,1)S(1)} %copy-done.5), kind=kOutput, calls=%fused_computation.33 | convolution fusion | flops 67108864 | bytes 2097152 | tf_op jit(solution)/shard_map/kab,kbf->kaf/dot_general | solution.py:44
  86.8 2.6 %copy.49 = f32[16,128,128]{2,0,1:T(8,128)} copy(f32[16,128,128]{1,2,0:T(8,128)} %convolution_bitcast_fusion.1) | data formatting | bytes 2097152 | tf_op jit(solution)/shard_map/kab,kbf->kaf/dot_general | solution.py:44
  89.4 2.0 fusion.63
  91.4 1.9 fusion.43
  93.3 4.3 %gather_fusion.3 = bf16[1024,128]{1,0:T(8,128)(2,1)} fusion(bf16[2048,128]{1,0:T(8,128)(2,1)S(1)} %bitcast.138, s32[1024]{0:T(1024)S(1)} %fusion.70), kind=kCustom, calls=%fused_computation.1.clone | custom fusion | bytes 528384 | tf_op jit(solution)/shard_map/jit(_take)/gather | solution.py:90
  98.6 2.5 %convolution_bitcast_fusion = f32[16,128,128]{1,2,0:T(8,128)} fusion(bf16[16,128,128]{2,1,0:T(8,128)(2,1)} %all-to-all-done.3, bf16[16,128,128]{2,1,0:T(8,128)(2,1)S(1)} %copy-done.6), kind=kOutput, calls=%fused_computation.32 | convolution fusion | flops 67108864 | bytes 2097152 | tf_op jit(solution)/shard_map/kab,kbf->kaf/dot_general | solution.py:44
  101.1 2.6 %copy.60 = f32[16,128,128]{2,0,1:T(8,128)} copy(f32[16,128,128]{1,2,0:T(8,128)} %convolution_bitcast_fusion) | data formatting | bytes 2097152 | tf_op jit(solution)/shard_map/kab,kbf->kaf/dot_general | solution.py:44
  103.8 2.0 fusion.61
  105.8 1.8 fusion.38
  107.7 3.2 %gather_fusion.5 = bf16[1024,128]{1,0:T(8,128)(2,1)S(1)} fusion(bf16[2048,128]{1,0:T(8,128)(2,1)S(1)} %bitcast.140, s32[1024]{0:T(1024)S(1)} %fusion.70), kind=kCustom, calls=%fused_computation.5.clone | custom fusion | bytes 528384 | tf_op jit(solution)/shard_map/jit(_take)/gather | solution.py:92
  111.9 4.6 %all_to_all.45 = bf16[3,1024,128]{2,0,1:T(4,128)(2,1)S(1)} all-to-all(bf16[3,1024,128]{2,0,1:T(4,128)(2,1)S(1)} %copy.62), channel_id=1, replica_groups=mesh['band'=16,'dp'=2] {'dp'}, dimensions={1} | all-to-all | bytes 1572864 | tf_op jit(solution)/shard_map/all_to_all | solution.py:96
  119.1 2.5 %fusion.3 = (bf16[512,1024]{1,0:T(8,128)(2,1)S(1)}, f32[512,1024,1]{1,0,2:T(8,128)}) fusion(bf16[3,512,256]{2,1,0:T(8,128)(2,1)S(1)} %all_to_all.39, bf16[3,256,1024]{2,1,0:T(8,128)(2,1)S(1)} %bitcast.129), kind=kOutput, calls=%fused_computation.12 | convolution fusion | flops 807927808 | bytes 5505024 | tf_op jit(solution)/shard_map/krf,kfh->rh/dot_general | solution.py:99
  122.9 5.4 %fusion.21 = f32[768,1024]{1,0:T(8,128)} fusion(bf16[768,512]{1,0:T(8,128)(2,1)} %bitcast.145, f32[512,1024,1]{1,0,2:T(8,128)} %get-tuple-element.83, bf16[1024,256]{1,0:T(8,128)(2,1)} %param.31, f32[512,256]{0,1:T(8,128)S(1)} %get-tuple-element.85, s32[512]{0:T(512)S(1)} %copy-done.19, f32[512]{0:T(512)S(1)} %fusion.56, f32[512]{0:T(512)S(1)} %get-tuple-element.84), kind=kOutput, calls=%fused_computation.30 | convolution fusion | flops 1079377920 | bytes 7084032 | tf_op jit(solution)/shard_map/krf,rh->kfh/dot_general | solution.py:115
  128.3 93.5 %all-reduce.3 = (bf16[768,1024]{1,0:T(8,128)(2,1)}, bf16[1024,256]{1,0:T(8,128)(2,1)}) all-reduce(f32[768,1024]{1,0:T(8,128)} %fusion.21, f32[1024,256]{1,0:T(8,128)S(1)} %fusion.75), channel_id=1, replica_groups=mesh['band'=16,'dp'=2] {'band','dp'}, use_global_device_ids=true, to_apply=%region_2.5 | all-reduce | flops 1048576 | bytes 6291456 | tf_op jit(solution)/shard_map/psum | solution.py:118
  (86 shorter events, 21.9 us)
Async XLA Ops:
  0.6 118.5 %copy-start = (bf16[768,1024]{1,0:T(8,128)(2,1)S(1)}, bf16[768,1024]{1,0:T(8,128)(2,1)}, u32[]{:S(2)}) copy-start(bf16[768,1024]{1,0:T(8,128)(2,1)} %param.30) | copy-start | bytes 4718596
  2.1 29.8 %all-to-all-start = ((s32[16,1,1]{2,1,0:T(1,128)}), s32[16,1,1]{2,1,0:T(1,128)S(1)}, u32[]{:S(2)}, u32[]{:S(2)}) async-start(s32[16,1,1]{2,1,0:T(1,128)} %copy.47), calls=%async_computation | async-start | bytes 16384 | tf_op jit(solution)/shard_map/all_to_all | solution.py:31
  11.2 37.6 %collective-permute-start = (bf16[128,128]{1,0:T(8,128)(2,1)S(1)}, bf16[128,128]{1,0:T(8,128)(2,1)S(1)}, u32[]{:S(2)}, u32[]{:S(2)}) collective-permute-start(bf16[128,128]{1,0:T(8,128)(2,1)S(1)} %get-tuple-element.77), channel_id=1, source_target_pairs={{0,2},{2,4},{4,6},{6,8},{8,10},{10,12},{12,14},{14,16},{16,18},{18... | collective-permute-start | bytes 98312 | tf_op jit(solution)/shard_map/ppermute | solution.py:15
  15.0 33.8 %collective-permute-start.1 = (bf16[128,128]{1,0:T(8,128)(2,1)S(1)}, bf16[128,128]{1,0:T(8,128)(2,1)S(1)}, u32[]{:S(2)}, u32[]{:S(2)}) collective-permute-start(bf16[128,128]{1,0:T(8,128)(2,1)S(1)} %get-tuple-element.78), channel_id=1, source_target_pairs={{2,0},{4,2},{6,4},{8,6},{10,8},{12,10},{14,12},{16,14},{18,16},{20... | collective-permute-start | bytes 98312 | tf_op jit(solution)/shard_map/ppermute | solution.py:17
  18.9 4.8 %copy-start.16 = (s32[16]{0:T(128)S(1)}, s32[16]{0:T(128)}, u32[]{:S(2)}) copy-start(s32[16]{0:T(128)} %param.26) | copy-start | bytes 196
  19.0 5.3 %copy-start.14 = (s32[1024]{0:T(1024)S(1)}, s32[1024]{0:T(1024)}, u32[]{:S(2)}) copy-start(s32[1024]{0:T(1024)} %param.28) | copy-start | bytes 12292
  19.0 6.0 %copy-start.2 = (bf16[2048,128]{1,0:T(8,128)(2,1)S(1)}, bf16[2048,128]{1,0:T(8,128)(2,1)}, u32[]{:S(2)}) copy-start(bf16[2048,128]{1,0:T(8,128)(2,1)} %param.23) | copy-start | bytes 1572868
  19.1 27.7 %collective-permute-start.2 = (f32[128,128]{1,0:T(8,128)S(1)}, f32[128,128]{1,0:T(8,128)S(1)}, u32[]{:S(2)}, u32[]{:S(2)}) collective-permute-start(f32[128,128]{1,0:T(8,128)S(1)} %slice_bitcast_fusion.4), channel_id=1, source_target_pairs={{0,2},{2,4},{4,6},{6,8},{8,10},{10,12},{12,14},{14,16},{16,18},{18... | collective-permute-start | bytes 196616 | tf_op jit(solution)/shard_map/ppermute | solution.py:15
  31.9 23.3 %all-to-all-start.2 = ((bf16[16,128,128]{2,1,0:T(8,128)(2,1)}), bf16[16,128,128]{2,1,0:T(8,128)(2,1)}, u32[]{:S(2)}, u32[]{:S(2)}) async-start(bf16[16,128,128]{2,1,0:T(8,128)(2,1)} %copy.55), calls=%async_computation.2 | async-start | bytes 1048576 | tf_op jit(solution)/shard_map/all_to_all | solution.py:74
  44.9 18.0 %copy-start.18 = (s32[16]{0:T(128)S(1)}, s32[16]{0:T(128)}, u32[]{:S(2)}) copy-start(s32[16]{0:T(128)} %reduce.10) | copy-start | bytes 196
  47.5 6.1 %collective-permute-start.3 = (f32[128,128]{1,0:T(8,128)S(1)}, f32[128,128]{1,0:T(8,128)S(1)}, u32[]{:S(2)}, u32[]{:S(2)}) collective-permute-start(f32[128,128]{1,0:T(8,128)S(1)} %get-tuple-element.69), channel_id=1, source_target_pairs={{2,0},{4,2},{6,4},{8,6},{10,8},{12,10},{14,12},{16,14},{18,16},{20... | collective-permute-start | bytes 196616 | tf_op jit(solution)/shard_map/ppermute | solution.py:17
  55.1 21.4 %all-to-all-start.1 = ((bf16[16,128,128]{1,2,0:T(8,128)(2,1)}), bf16[16,128,128]{1,2,0:T(8,128)(2,1)}, u32[]{:S(2)}, u32[]{:S(2)}) async-start(bf16[16,128,128]{1,2,0:T(8,128)(2,1)} %broadcast_select_fusion.1), calls=%async_computation.1 | async-start | bytes 1048576 | tf_op jit(solution)/shard_map/all_to_all | solution.py:73
  63.0 1.5 copy-start.7
  64.9 40.9 %copy-start.1 = (bf16[16,128,128]{2,1,0:T(8,128)(2,1)}, bf16[16,128,128]{2,1,0:T(8,128)(2,1)S(1)}, u32[]{:S(2)}) copy-start(bf16[16,128,128]{2,1,0:T(8,128)(2,1)S(1)} %fusion.50) | copy-start | bytes 1572868
  66.3 31.3 %collective-permute-start.4 = (bf16[128,128]{1,0:T(8,128)(2,1)S(1)}, bf16[128,128]{1,0:T(8,128)(2,1)S(1)}, u32[]{:S(2)}, u32[]{:S(2)}) collective-permute-start(bf16[128,128]{1,0:T(8,128)(2,1)S(1)} %get-tuple-element.73), channel_id=1, source_target_pairs={{0,2},{2,4},{4,6},{6,8},{8,10},{10,12},{12,14},{14,16},{16,18},{18... | collective-permute-start | bytes 98312 | tf_op jit(solution)/shard_map/ppermute | solution.py:15
  70.1 27.5 %collective-permute-start.5 = (bf16[128,128]{1,0:T(8,128)(2,1)S(1)}, bf16[128,128]{1,0:T(8,128)(2,1)S(1)}, u32[]{:S(2)}, u32[]{:S(2)}) collective-permute-start(bf16[128,128]{1,0:T(8,128)(2,1)S(1)} %get-tuple-element.74), channel_id=1, source_target_pairs={{2,0},{4,2},{6,4},{8,6},{10,8},{12,10},{14,12},{16,14},{18,16},{20... | collective-permute-start | bytes 98312 | tf_op jit(solution)/shard_map/ppermute | solution.py:17
  71.4 12.9 %copy-start.5 = (bf16[16,128,128]{2,1,0:T(8,128)(2,1)S(1)}, bf16[16,128,128]{2,1,0:T(8,128)(2,1)}, u32[]{:S(2)}) copy-start(bf16[16,128,128]{2,1,0:T(8,128)(2,1)} %param.25) | copy-start | bytes 1572868
  76.6 22.0 %all-to-all-start.3 = ((bf16[16,128,128]{2,1,0:T(8,128)(2,1)}), bf16[16,128,128]{2,1,0:T(8,128)(2,1)}, u32[]{:S(2)}, u32[]{:S(2)}) async-start(bf16[16,128,128]{2,1,0:T(8,128)(2,1)} %broadcast_select_fusion), calls=%async_computation.3 | async-start | bytes 1048576 | tf_op jit(solution)/shard_map/all_to_all | solution.py:80
  84.3 5.1 %copy-start.17 = (s32[16]{0:T(128)S(1)}, s32[16]{0:T(128)}, u32[]{:S(2)}) copy-start(s32[16]{0:T(128)} %param.26) | copy-start | bytes 196
  89.4 2.0 copy-start.8
  89.4 2.0 copy-start.12
  93.3 7.9 %copy-start.3 = (bf16[16,128,128]{2,1,0:T(8,128)(2,1)}, bf16[16,128,128]{2,1,0:T(8,128)(2,1)S(1)}, u32[]{:S(2)}) copy-start(bf16[16,128,128]{2,1,0:T(8,128)(2,1)S(1)} %fusion.43) | copy-start | bytes 1572868
  93.3 5.3 %copy-start.6 = (bf16[16,128,128]{2,1,0:T(8,128)(2,1)S(1)}, bf16[16,128,128]{2,1,0:T(8,128)(2,1)}, u32[]{:S(2)}) copy-start(bf16[16,128,128]{2,1,0:T(8,128)(2,1)} %param.25) | copy-start | bytes 1572868
  103.8 2.0 copy-start.9
  103.8 2.0 copy-start.13
  107.6 3.6 %copy-start.4 = (bf16[16,128,128]{2,1,0:T(8,128)(2,1)}, bf16[16,128,128]{2,1,0:T(8,128)(2,1)S(1)}, u32[]{:S(2)}) copy-start(bf16[16,128,128]{2,1,0:T(8,128)(2,1)S(1)} %fusion.38) | copy-start | bytes 1572868
  107.6 3.2 %copy-start.10 = (bf16[1024,128]{1,0:T(8,128)(2,1)S(1)}, bf16[1024,128]{1,0:T(8,128)(2,1)}, u32[]{:S(2)}) copy-start(bf16[1024,128]{1,0:T(8,128)(2,1)} %gather_fusion.3) | copy-start | bytes 786436
  107.7 3.2 %copy-start.15 = (pred[1024]{0:T(1024)(128)(4,1)S(1)}, pred[1024]{0:T(1024)(128)(4,1)}, u32[]{:S(2)}) copy-start(pred[1024]{0:T(1024)(128)(4,1)} %compare_and_fusion) | copy-start | bytes 3076
  119.1 2.5 %copy-start.11 = (bf16[1024,256]{1,0:T(8,128)(2,1)S(1)}, bf16[1024,256]{1,0:T(8,128)(2,1)}, u32[]{:S(2)}) copy-start(bf16[1024,256]{1,0:T(8,128)(2,1)} %param.31) | copy-start | bytes 1572868
  121.6 0.7 copy-start.19
where the time goes:
time: 223 us; the launch traced here: 222 us
  blocking collectives  98 us (44%)
  starting transfers between devices  47.2 us (21%)
  local copies, waits for them, and re-layouts  31.2 us (14%)
  matrix products  27.8 us (12%)
  other arithmetic  12.6 us (6%)
  waiting for transfers between devices  3.83 us (2%)
    psum x1, blocking collectives, per_device(): lax.psum((grad_first, grad_second), ('band', 'dp'))  93.5 us
    ppermute x3, starting transfers between devices, padded_2(): lax.ppermute(tail, axis, [(i, (i + 1) % count) for i in range(ends)])  12.1 us
    all_to_all x1, starting transfers between devices, per_device(): lax.all_to_all(requests, 'band', split_axis=0, concat_axis=0, tiled=True)  8.31 us
    all_to_all x1, starting transfers between devices, per_device(): lax.all_to_all(outgoing, 'band', split_axis=0, concat_axis=0, tiled=True)  7.81 us
    all_to_all x1, starting transfers between devices, per_device(): lax.all_to_all(serve_blocks(prop_t), 'band', split_axis=0, concat_axis=0,...  7.68 us
    all_to_all x1, starting transfers between devices, per_device(): lax.all_to_all(back_terms, 'band', split_axis=0, concat_axis=0, tiled=True)  7.4 us
    dot_general x1, matrix products, per_device(): jnp.einsum('krf,rh->kfh', regrouped, back_signal, preferred_element_type=...  5.42 us
    dot_general x2, local copies, waits for them, and re-layouts, off_apply(): jnp.einsum('kab,kbf->kaf', off_tiles, fetched, preferred_element_type=jnp...  5.22 us
  transfers between devices with their start and end apart: 10, of which 1 were waited for; matrix products, arithmetic and copies ran while one was open for 20% of the time, Pallas kernels for 0%

commit v1 on v0

--- a/solution.py
+++ b/solution.py
@@ -115,7 +115,7 @@
     grad_first = jnp.einsum(
         "krf,rh->kfh", regrouped, back_signal, preferred_element_type=jnp.float32
     ).reshape(w_first.shape[0], hidden_units)
-    summed_first, summed_second = lax.psum((grad_first, grad_second), ("band", "dp"))
+    summed_first, summed_second = lax.psum(lax.psum((grad_first, grad_second), "dp"), "band")
     return (
         prop_a,
         prop_t,

time: 223 us -> 354 us (1.59)
  blocking collectives: 98 us -> 185 us
  waiting for transfers between devices: 3.83 us -> 33.8 us
  between operations: 1.12 us -> 14.5 us
    psum x1, blocking collectives: 93.5 us -> 181 us  [per_device(): lax.psum(lax.psum((grad_first, grad_second), 'dp'), 'band')]
    psum x0 -> x1, waiting for transfers between devices: none -> 30 us  [per_device(): lax.psum((grad_first, grad_second), 'dp')]
  transfers between devices with their start and end apart: 10 -> 11, of which waited for: 1 -> 2; matrix products, arithmetic and copies ran while one was open for 20% -> 13% of each run, Pallas kernels for 0% -> 0%
where the time goes in v1:
time: 354 us; the launch traced here: 353 us
  blocking collectives  185 us (52%)
  starting transfers between devices  47.2 us (13%)
  waiting for transfers between devices  33.8 us (10%)
  local copies, waits for them, and re-layouts  31.2 us (9%)
  matrix products  28.3 us (8%)
  between operations  14.5 us (4%)
  other arithmetic  12.4 us (4%)
    psum x1, blocking collectives, per_device(): lax.psum(lax.psum((grad_first, grad_second), 'dp'), 'band')  181 us
    psum x1, waiting for transfers between devices, per_device(): lax.psum((grad_first, grad_second), 'dp')  30 us
    ppermute x3, starting transfers between devices, padded_2(): lax.ppermute(tail, axis, [(i, (i + 1) % count) for i in range(ends)])  12.1 us
    all_to_all x1, starting transfers between devices, per_device(): lax.all_to_all(requests, 'band', split_axis=0, concat_axis=0, tiled=True)  8.31 us
    all_to_all x1, starting transfers between devices, per_device(): lax.all_to_all(outgoing, 'band', split_axis=0, concat_axis=0, tiled=True)  7.81 us
    all_to_all x1, starting transfers between devices, per_device(): lax.all_to_all(serve_blocks(prop_t), 'band', split_axis=0, concat_axis=0,...  7.68 us
    all_to_all x1, starting transfers between devices, per_device(): lax.all_to_all(back_terms, 'band', split_axis=0, concat_axis=0, tiled=True)  7.4 us
  transfers between devices with their start and end apart: 11, of which 2 were waited for; matrix products, arithmetic and copies ran while one was open for 13% of the time, Pallas kernels for 0%

profile of v1, /device:TPU:0, one launch (start us, length us, event | category | flops | bytes accessed | tf_op | source)
XLA Modules:
  0.0 352.8 jit_solution(3209450561910589567)
XLA Ops:
  8.6 8.3 %all-to-all-start = ((s32[16,1,1]{2,1,0:T(1,128)}), s32[16,1,1]{2,1,0:T(1,128)S(1)}, u32[]{:S(2)}, u32[]{:S(2)}) async-start(s32[16,1,1]{2,1,0:T(1,128)} %copy.47), calls=%async_computation | async-start | bytes 16384 | tf_op jit(solution)/shard_map/all_to_all | solution.py:31
  17.7 3.8 %collective-permute-start = (bf16[128,128]{1,0:T(8,128)(2,1)S(1)}, bf16[128,128]{1,0:T(8,128)(2,1)S(1)}, u32[]{:S(2)}, u32[]{:S(2)}) collective-permute-start(bf16[128,128]{1,0:T(8,128)(2,1)S(1)} %get-tuple-element.79), channel_id=1, source_target_pairs={{0,2},{2,4},{4,6},{6,8},{8,10},{10,12},{12,14},{14,16},{16,18},{18... | collective-permute-start | bytes 98312 | tf_op jit(solution)/shard_map/ppermute | solution.py:15
  22.9 2.1 fusion.78
  25.7 4.5 %collective-permute-start.2 = (f32[128,128]{1,0:T(8,128)S(1)}, f32[128,128]{1,0:T(8,128)S(1)}, u32[]{:S(2)}, u32[]{:S(2)}) collective-permute-start(f32[128,128]{1,0:T(8,128)S(1)} %slice_bitcast_fusion.4), channel_id=1, source_target_pairs={{0,2},{2,4},{4,6},{6,8},{8,10},{10,12},{12,14},{14,16},{16,18},{18... | collective-permute-start | bytes 196616 | tf_op jit(solution)/shard_map/ppermute | solution.py:15
  32.8 2.4 fusion.46
  35.3 2.0 copy.55
  38.4 7.4 %all-to-all-start.2 = ((bf16[16,128,128]{2,1,0:T(8,128)(2,1)}), bf16[16,128,128]{2,1,0:T(8,128)(2,1)}, u32[]{:S(2)}, u32[]{:S(2)}) async-start(bf16[16,128,128]{2,1,0:T(8,128)(2,1)} %copy.55), calls=%async_computation.2 | async-start | bytes 1048576 | tf_op jit(solution)/shard_map/all_to_all | solution.py:74
  49.2 2.0 copy.48
  51.2 1.9 broadcast_select_fusion.1
  56.2 3.8 %collective-permute-done.3 = f32[128,128]{1,0:T(8,128)S(1)} collective-permute-done((f32[128,128]{1,0:T(8,128)S(1)}, f32[128,128]{1,0:T(8,128)S(1)}, u32[]{:S(2)}, u32[]{:S(2)}) %collective-permute-start.3) | collective-permute-done | bytes 65568 | tf_op jit(solution)/shard_map/ppermute | solution.py:17
  61.5 7.8 %all-to-all-start.1 = ((bf16[16,128,128]{1,2,0:T(8,128)(2,1)}), bf16[16,128,128]{1,2,0:T(8,128)(2,1)}, u32[]{:S(2)}, u32[]{:S(2)}) async-start(bf16[16,128,128]{1,2,0:T(8,128)(2,1)} %broadcast_select_fusion.1), calls=%async_computation.1 | async-start | bytes 1048576 | tf_op jit(solution)/shard_map/all_to_all | solution.py:73
  69.3 1.5 fusion.52
  72.6 3.8 %collective-permute-start.4 = (bf16[128,128]{1,0:T(8,128)(2,1)S(1)}, bf16[128,128]{1,0:T(8,128)(2,1)S(1)}, u32[]{:S(2)}, u32[]{:S(2)}) collective-permute-start(bf16[128,128]{1,0:T(8,128)(2,1)S(1)} %get-tuple-element.75), channel_id=1, source_target_pairs={{0,2},{2,4},{4,6},{6,8},{8,10},{10,12},{12,14},{14,16},{16,18},{18... | collective-permute-start | bytes 98312 | tf_op jit(solution)/shard_map/ppermute | solution.py:15
  77.7 3.2 gather_fusion.4
  80.9 2.0 broadcast_select_fusion
  82.9 7.7 %all-to-all-start.3 = ((bf16[16,128,128]{2,1,0:T(8,128)(2,1)}), bf16[16,128,128]{2,1,0:T(8,128)(2,1)}, u32[]{:S(2)}, u32[]{:S(2)}) async-start(bf16[16,128,128]{2,1,0:T(8,128)(2,1)} %broadcast_select_fusion), calls=%async_computation.3 | async-start | bytes 1048576 | tf_op jit(solution)/shard_map/all_to_all | solution.py:80
  90.6 2.5 convolution_bitcast_fusion.1
  93.1 2.6 copy.49
  95.8 2.0 fusion.63
  97.8 1.9 fusion.43
  99.7 4.3 %gather_fusion.3 = bf16[1024,128]{1,0:T(8,128)(2,1)} fusion(bf16[2048,128]{1,0:T(8,128)(2,1)S(1)} %bitcast.138, s32[1024]{0:T(1024)S(1)} %fusion.70), kind=kCustom, calls=%fused_computation.1.clone | custom fusion | bytes 528384 | tf_op jit(solution)/shard_map/jit(_take)/gather | solution.py:90
  105.0 2.5 convolution_bitcast_fusion
  107.5 2.6 copy.60
  110.1 2.0 fusion.61
  112.1 1.9 fusion.38
  114.0 3.2 gather_fusion.5
  118.3 4.6 %all_to_all.45 = bf16[3,1024,128]{2,0,1:T(4,128)(2,1)S(1)} all-to-all(bf16[3,1024,128]{2,0,1:T(4,128)(2,1)S(1)} %copy.62), channel_id=1, replica_groups=mesh['band'=16,'dp'=2] {'dp'}, dimensions={1} | all-to-all | bytes 1572864 | tf_op jit(solution)/shard_map/all_to_all | solution.py:96
  125.5 2.5 fusion.3
  128.7 1.5 fusion.75
  130.2 5.0 %fusion.21 = f32[768,1024]{1,0:T(8,128)} fusion(bf16[768,512]{1,0:T(8,128)(2,1)S(1)} %bitcast.145, f32[512,1024,1]{1,0,2:T(8,128)} %get-tuple-element.85, bf16[1024,256]{1,0:T(8,128)(2,1)S(1)} %copy-done.13, f32[512,256]{0,1:T(8,128)S(1)} %get-tuple-element.87, s32[512]{0:T(512)S(1)} %copy-done.21, f32[512]{0:T(512)S(1)} %fusion.56, ...), kind=kOutput, calls=%fused_computation.30 | convolution fusion | flops 1079377920 | bytes 7084032 | tf_op jit(solution)/shard_map/krf,rh->kfh/dot_general | solution.py:115
  135.2 30.0 %all-reduce.6.cloned.1.call-done = (f32[768,1024]{1,0:T(8,128)}, f32[1024,256]{1,0:T(8,128)}) async-done(((f32[768,1024]{1,0:T(8,128)}, f32[1024,256]{1,0:T(8,128)}), (f32[768,1024]{1,0:T(8,128)}, f32[1024,256]{1,0:T(8,128)})) %all-reduce.6.cloned.1.call-update) | async-done | bytes 4194320 | tf_op jit(solution)/shard_map/psum | solution.py:118
  165.2 180.7 %all-reduce.7 = (bf16[768,1024]{1,0:T(8,128)(2,1)}, bf16[1024,256]{1,0:T(8,128)(2,1)}) all-reduce(f32[768,1024]{1,0:T(8,128)} %get-tuple-element.69, f32[1024,256]{1,0:T(8,128)} %get-tuple-element.70), channel_id=1, replica_groups=mesh['band'=16,'dp'=2] {'band'}, use_global_device_ids=true, to_apply=%region_3.6 | all-reduce | flops 1048576 | bytes 6291456 | tf_op jit(solution)/shard_map/psum | solution.py:118
  (93 shorter events, 24.1 us)
Async XLA Ops:
  7.2 118.3 %copy-start = (bf16[768,1024]{1,0:T(8,128)(2,1)S(1)}, bf16[768,1024]{1,0:T(8,128)(2,1)}, u32[]{:S(2)}) copy-start(bf16[768,1024]{1,0:T(8,128)(2,1)} %param.30) | copy-start | bytes 4718596
  8.6 29.7 %all-to-all-start = ((s32[16,1,1]{2,1,0:T(1,128)}), s32[16,1,1]{2,1,0:T(1,128)S(1)}, u32[]{:S(2)}, u32[]{:S(2)}) async-start(s32[16,1,1]{2,1,0:T(1,128)} %copy.47), calls=%async_computation | async-start | bytes 16384 | tf_op jit(solution)/shard_map/all_to_all | solution.py:31
  17.7 37.4 %collective-permute-start = (bf16[128,128]{1,0:T(8,128)(2,1)S(1)}, bf16[128,128]{1,0:T(8,128)(2,1)S(1)}, u32[]{:S(2)}, u32[]{:S(2)}) collective-permute-start(bf16[128,128]{1,0:T(8,128)(2,1)S(1)} %get-tuple-element.79), channel_id=1, source_target_pairs={{0,2},{2,4},{4,6},{6,8},{8,10},{10,12},{12,14},{14,16},{16,18},{18... | collective-permute-start | bytes 98312 | tf_op jit(solution)/shard_map/ppermute | solution.py:15
  21.6 33.6 %collective-permute-start.1 = (bf16[128,128]{1,0:T(8,128)(2,1)S(1)}, bf16[128,128]{1,0:T(8,128)(2,1)S(1)}, u32[]{:S(2)}, u32[]{:S(2)}) collective-permute-start(bf16[128,128]{1,0:T(8,128)(2,1)S(1)} %get-tuple-element.80), channel_id=1, source_target_pairs={{2,0},{4,2},{6,4},{8,6},{10,8},{12,10},{14,12},{16,14},{18,16},{20... | collective-permute-start | bytes 98312 | tf_op jit(solution)/shard_map/ppermute | solution.py:17
  25.5 4.8 %copy-start.18 = (s32[16]{0:T(128)S(1)}, s32[16]{0:T(128)}, u32[]{:S(2)}) copy-start(s32[16]{0:T(128)} %param.26) | copy-start | bytes 196
  25.5 5.3 %copy-start.16 = (s32[1024]{0:T(1024)S(1)}, s32[1024]{0:T(1024)}, u32[]{:S(2)}) copy-start(s32[1024]{0:T(1024)} %param.28) | copy-start | bytes 12292
  25.5 5.9 %copy-start.2 = (bf16[2048,128]{1,0:T(8,128)(2,1)S(1)}, bf16[2048,128]{1,0:T(8,128)(2,1)}, u32[]{:S(2)}) copy-start(bf16[2048,128]{1,0:T(8,128)(2,1)} %param.23) | copy-start | bytes 1572868
  25.7 27.5 %collective-permute-start.2 = (f32[128,128]{1,0:T(8,128)S(1)}, f32[128,128]{1,0:T(8,128)S(1)}, u32[]{:S(2)}, u32[]{:S(2)}) collective-permute-start(f32[128,128]{1,0:T(8,128)S(1)} %slice_bitcast_fusion.4), channel_id=1, source_target_pairs={{0,2},{2,4},{4,6},{6,8},{8,10},{10,12},{12,14},{14,16},{16,18},{18... | collective-permute-start | bytes 196616 | tf_op jit(solution)/shard_map/ppermute | solution.py:15
  38.4 23.1 %all-to-all-start.2 = ((bf16[16,128,128]{2,1,0:T(8,128)(2,1)}), bf16[16,128,128]{2,1,0:T(8,128)(2,1)}, u32[]{:S(2)}, u32[]{:S(2)}) async-start(bf16[16,128,128]{2,1,0:T(8,128)(2,1)} %copy.55), calls=%async_computation.2 | async-start | bytes 1048576 | tf_op jit(solution)/shard_map/all_to_all | solution.py:74
  51.2 18.0 %copy-start.20 = (s32[16]{0:T(128)S(1)}, s32[16]{0:T(128)}, u32[]{:S(2)}) copy-start(s32[16]{0:T(128)} %reduce.10) | copy-start | bytes 196
  53.8 6.1 %collective-permute-start.3 = (f32[128,128]{1,0:T(8,128)S(1)}, f32[128,128]{1,0:T(8,128)S(1)}, u32[]{:S(2)}, u32[]{:S(2)}) collective-permute-start(f32[128,128]{1,0:T(8,128)S(1)} %get-tuple-element.71), channel_id=1, source_target_pairs={{2,0},{4,2},{6,4},{8,6},{10,8},{12,10},{14,12},{16,14},{18,16},{20... | collective-permute-start | bytes 196616 | tf_op jit(solution)/shard_map/ppermute | solution.py:17
  61.5 21.4 %all-to-all-start.1 = ((bf16[16,128,128]{1,2,0:T(8,128)(2,1)}), bf16[16,128,128]{1,2,0:T(8,128)(2,1)}, u32[]{:S(2)}, u32[]{:S(2)}) async-start(bf16[16,128,128]{1,2,0:T(8,128)(2,1)} %broadcast_select_fusion.1), calls=%async_computation.1 | async-start | bytes 1048576 | tf_op jit(solution)/shard_map/all_to_all | solution.py:73
  69.3 1.5 copy-start.7
  71.2 40.9 %copy-start.1 = (bf16[16,128,128]{2,1,0:T(8,128)(2,1)}, bf16[16,128,128]{2,1,0:T(8,128)(2,1)S(1)}, u32[]{:S(2)}) copy-start(bf16[16,128,128]{2,1,0:T(8,128)(2,1)S(1)} %fusion.50) | copy-start | bytes 1572868
  72.6 31.3 %collective-permute-start.4 = (bf16[128,128]{1,0:T(8,128)(2,1)S(1)}, bf16[128,128]{1,0:T(8,128)(2,1)S(1)}, u32[]{:S(2)}, u32[]{:S(2)}) collective-permute-start(bf16[128,128]{1,0:T(8,128)(2,1)S(1)} %get-tuple-element.75), channel_id=1, source_target_pairs={{0,2},{2,4},{4,6},{6,8},{8,10},{10,12},{12,14},{14,16},{16,18},{18... | collective-permute-start | bytes 98312 | tf_op jit(solution)/shard_map/ppermute | solution.py:15
  76.4 27.5 %collective-permute-start.5 = (bf16[128,128]{1,0:T(8,128)(2,1)S(1)}, bf16[128,128]{1,0:T(8,128)(2,1)S(1)}, u32[]{:S(2)}, u32[]{:S(2)}) collective-permute-start(bf16[128,128]{1,0:T(8,128)(2,1)S(1)} %get-tuple-element.76), channel_id=1, source_target_pairs={{2,0},{4,2},{6,4},{8,6},{10,8},{12,10},{14,12},{16,14},{18,16},{20... | collective-permute-start | bytes 98312 | tf_op jit(solution)/shard_map/ppermute | solution.py:17
  77.7 12.9 %copy-start.5 = (bf16[16,128,128]{2,1,0:T(8,128)(2,1)S(1)}, bf16[16,128,128]{2,1,0:T(8,128)(2,1)}, u32[]{:S(2)}) copy-start(bf16[16,128,128]{2,1,0:T(8,128)(2,1)} %param.25) | copy-start | bytes 1572868
  82.9 22.1 %all-to-all-start.3 = ((bf16[16,128,128]{2,1,0:T(8,128)(2,1)}), bf16[16,128,128]{2,1,0:T(8,128)(2,1)}, u32[]{:S(2)}, u32[]{:S(2)}) async-start(bf16[16,128,128]{2,1,0:T(8,128)(2,1)} %broadcast_select_fusion), calls=%async_computation.3 | async-start | bytes 1048576 | tf_op jit(solution)/shard_map/all_to_all | solution.py:80
  90.6 5.2 %copy-start.19 = (s32[16]{0:T(128)S(1)}, s32[16]{0:T(128)}, u32[]{:S(2)}) copy-start(s32[16]{0:T(128)} %param.26) | copy-start | bytes 196
  90.6 74.6 %all-reduce.6.cloned.1.call-start = ((), (), s32[]{:S(2)}) async-start(), calls=%async_computation.5 | async-start | bytes 8388608 | tf_op jit(solution)/shard_map/psum | solution.py:118
  95.7 2.0 copy-start.8
  95.7 2.0 copy-start.14
  99.6 7.9 %copy-start.3 = (bf16[16,128,128]{2,1,0:T(8,128)(2,1)}, bf16[16,128,128]{2,1,0:T(8,128)(2,1)S(1)}, u32[]{:S(2)}) copy-start(bf16[16,128,128]{2,1,0:T(8,128)(2,1)S(1)} %fusion.43) | copy-start | bytes 1572868
  99.6 5.3 %copy-start.6 = (bf16[16,128,128]{2,1,0:T(8,128)(2,1)S(1)}, bf16[16,128,128]{2,1,0:T(8,128)(2,1)}, u32[]{:S(2)}) copy-start(bf16[16,128,128]{2,1,0:T(8,128)(2,1)} %param.25) | copy-start | bytes 1572868
  110.1 2.0 copy-start.9
  110.1 2.0 copy-start.15
  114.0 3.6 %copy-start.4 = (bf16[16,128,128]{2,1,0:T(8,128)(2,1)}, bf16[16,128,128]{2,1,0:T(8,128)(2,1)S(1)}, u32[]{:S(2)}) copy-start(bf16[16,128,128]{2,1,0:T(8,128)(2,1)S(1)} %fusion.38) | copy-start | bytes 1572868
  114.0 3.2 copy-start.10
  114.0 3.2 copy-start.17
  125.5 2.5 copy-start.12
  128.5 1.7 copy-start.11
  128.5 1.7 copy-start.13
  (1 other events, 0.7 us)
Sparse Core Ops, SparseCore 0:
  135.4 29.8 all-reduce.5
